TPU v7x, 256 devices: a whole 4x4x8 slice. The times are simulated.
256 devices in a mesh: rows: 8 (over x, core), cols: 32 (over y, z).
Axes of the slice: x: 4, y: 4, z: 8, core: 2. Of those that a mesh axis runs over, the one named last changes fastest.
Arguments:
- image: bfloat16 [256, 256, 192], P('rows', 'cols'), may hold values from -6 to 6
- in_weight: bfloat16 [192, 768], replicated, may hold values from -0.4375 to 0.4375
- conv_weight: float32 [3, 3, 384], replicated, may hold values from -2 to 2
- conv_bias: float32 [384], replicated, may hold values from -3 to 3
- proj_weight: bfloat16 [4, 384, 44], replicated, may hold values from -0.3125 to 0.3125
- dt_weight: float32 [4, 12, 384], replicated, may hold values from -1.75 to 1.75
- dt_bias: float32 [4, 384], replicated, may hold values from -11 to -2.9
- a_log: float32 [4, 16, 384], replicated, may hold values from -0.7 to 2
- skip_gain: float32 [4, 384], replicated, may hold values from 0.05 to 0.5
- out_weight: bfloat16 [384, 192], replicated, may hold values from -0.3125 to 0.3125
Outputs:
- mixed: bfloat16 [256, 256, 192], P('rows', 'cols')
All inputs are finite; a program needn't handle non-finite values.
Results may differ from a plain program's by a relative error of at most 0.012.
Values may be sent and summed in bfloat16 or wider, within the bound.
A program may use at most 192 MiB of HBM per device.

v0:
```python
import functools
import math

import jax
import jax.numpy as jnp
from jax import lax
from jax.experimental import pallas as pl
from jax.experimental.pallas import tpu as pltpu
from jax.sharding import PartitionSpec as P

EPS = 1e-5
LOG2E = 1.0 / math.log(2.0)
MESH = pl.DeviceIdType.MESH
F32 = jnp.float32
BF16 = jnp.bfloat16
NR, NC = 8, 32
TR, TC = 32, 8
T = 256
E = 384
N = 16
RANK = 12
BL = 16
NB = T // BL


def norm_rows(v):
    centre = v - jnp.mean(v, axis=-1, keepdims=True)
    spread = jnp.mean(centre * centre, axis=-1, keepdims=True)
    return centre * lax.rsqrt(spread + EPS)


def silu(v):
    return v / (1.0 + jnp.exp(-v))


def softplus(v):
    return jnp.maximum(v, 0.0) + jnp.log1p(jnp.exp(-jnp.abs(v)))


def iota(shape, dim):
    return lax.broadcasted_iota(jnp.int32, shape, dim)


def kernel(
    img3, img2, win_h, cw_h, cb_h, proj_h, dtw_h, dtb_h, alog_h, skip_h, wout_h,
    out_ref,
    imgv, win, cw, cb, proj, dtw, dtb, alog, skip, wout,
    ecol, hal, xc, xl, xr, lh, rh, gate, tbuf, sval,
    sa, sc, rl, cl, rout, cout, rres, cres,
    linef, dts, us, bts, cms, hst, ys, tb2, imgf,
    wsem, hss, hrs, rss, rrs, css, crs, rss2, rrs2, css2, crs2,
):
    r = lax.axis_index("rows")
    c = lax.axis_index("cols")

    def col(k):
        return lax.rem(c + k + NC, NC)

    def row(k):
        return lax.rem(r + k + NR, NR)

    barrier = pltpu.get_barrier_semaphore()

    def hello(dr, dc):
        pl.semaphore_signal(barrier, inc=1, device_id=(dr, dc), device_id_type=MESH)

    def greet_cols(j, x):
        hello(r, col(j))
        return x

    def greet_rows(j, x):
        hello(row(j), c)
        return x

    lax.fori_loop(1, NC, greet_cols, 0)
    lax.fori_loop(1, NR, greet_rows, 0)
    for dr in (-1, 1):
        for dc in (-1, 1):
            hello(row(dr), col(dc))

    pairs = ((img2, imgv), (win_h, win), (cw_h, cw), (cb_h, cb), (proj_h, proj), (dtw_h, dtw),
             (dtb_h, dtb), (alog_h, alog), (skip_h, skip), (wout_h, wout))
    loads = [pltpu.make_async_copy(s, d, wsem.at[i]) for i, (s, d) in enumerate(pairs)]
    for load in loads:
        load.start()

    loads[0].wait()
    pixels = imgv[...].astype(F32)
    rest = pixels.shape[1] - 128
    imgf[0] = pixels[:, :128]
    imgf[1, :, pl.ds(0, rest)] = pixels[:, 128:]
    for side in (0, 1):
        at = pl.ds(side * (TC - 1), TR, stride=TC)
        edge = jnp.concatenate([imgf[0, at, :], imgf[1, at, :]], axis=1)[:, : 128 + rest]
        for k in range(4):
            ecol[side * 4 + k] = edge[k * 8 : (k + 1) * 8].astype(BF16)

    loads[1].wait()
    normed = norm_rows(pixels).astype(BF16)
    hidden = jnp.dot(normed, win[...], preferred_element_type=F32)
    xc[pl.ds(8, T), :] = hidden[:, :E].astype(BF16).astype(F32)
    gate[...] = silu(hidden[:, E:].astype(BF16).astype(F32))

    pl.semaphore_wait(barrier, (NC - 1) + (NR - 1) + 4)

    def halo(i, src, first, count, dr, dc):
        return pltpu.make_async_remote_copy(
            src_ref=src, dst_ref=hal.at[pl.ds(first, count)], send_sem=hss.at[i], recv_sem=hrs.at[i],
            device_id=(row(dr), col(dc)), device_id_type=MESH,
        )

    up, down = img3.at[pl.ds(0, 1)], img3.at[pl.ds(TR - 1, 1)]
    halos = [
        halo(0, ecol.at[pl.ds(4, 4)], 0, 4, 0, 1),
        halo(1, ecol.at[pl.ds(0, 4)], 4, 4, 0, -1),
        halo(2, down, 8, 1, 1, 0),
        halo(3, up, 9, 1, -1, 0),
        halo(4, down, 10, 1, 1, 1),
        halo(5, down, 11, 1, 1, -1),
        halo(6, up, 12, 1, -1, 1),
        halo(7, up, 13, 1, -1, -1),
    ]
    for copy in halos:
        copy.start()
    for copy in halos:
        copy.wait_recv()

    ring = jnp.concatenate([hal[k].astype(F32) for k in range(14)], axis=0)
    hin = jnp.dot(norm_rows(ring).astype(BF16), win[:, :E], preferred_element_type=F32)
    hin = hin.astype(BF16).astype(F32)
    has_l, has_r, has_u, has_d = c > 0, c < NC - 1, r > 0, r < NR - 1

    def kept(flag, v):
        return jnp.where(flag, v, jnp.zeros_like(v))

    lh[pl.ds(0, TR), :] = kept(has_l, hin[0:32])
    rh[pl.ds(0, TR), :] = kept(has_r, hin[32:64])
    xc[pl.ds(0, 8), :] = kept(has_u, hin[64:72])
    xc[pl.ds(8 + T, 8), :] = kept(has_d, hin[72:80])
    lh[pl.ds(32, 8), :] = kept(jnp.logical_and(has_u, has_l), hin[80:88])
    rh[pl.ds(32, 8), :] = kept(jnp.logical_and(has_u, has_r), hin[88:96])
    lh[pl.ds(40, 8), :] = kept(jnp.logical_and(has_d, has_l), hin[96:104])
    rh[pl.ds(40, 8), :] = kept(jnp.logical_and(has_d, has_r), hin[104:112])

    sub = iota((8, E), 0)

    def sides(q, lrow, rrow):
        at = pl.ds(pl.multiple_of(q * 8, 8), 8)
        v = xc[at, :]
        xl[at, :] = jnp.where(sub == 0, jnp.broadcast_to(lh[pl.ds(lrow, 1), :], (8, E)), pltpu.roll(v, 1, 0))
        xr[at, :] = jnp.where(sub == 7, jnp.broadcast_to(rh[pl.ds(rrow, 1), :], (8, E)), pltpu.roll(v, 7, 0))

    def all_sides(q, x):
        sides(q + 1, q, q)
        return x

    sides(0, 39, 32)
    sides(TR + 1, 47, 40)
    lax.fori_loop(0, TR, all_sides, 0, unroll=4)

    loads[2].wait()
    loads[3].wait()

    def conv(q, x):
        acc = jnp.broadcast_to(cb[...], (8, E))
        for i in range(3):
            at = pl.ds(pl.multiple_of((q + i) * 8, 8), 8)
            for j, ref in enumerate((xl, xc, xr)):
                acc = acc + ref[at, :] * cw[i, j : j + 1, :]
        s = silu(acc).astype(BF16)
        sa[q] = s
        sf = s.astype(F32)
        sval[pl.ds(pl.multiple_of(q * 8, 8), 8), :] = sf
        for k in range(3):
            tbuf[k, pl.ds(q, 8, stride=TR), :] = sf[:, k * 128 : (k + 1) * 128]
        return x

    lax.fori_loop(0, TR, conv, 0, unroll=2)
    for j in range(TC):
        for k in range(3):
            sc[j, :, pl.ds(k * 128, 128)] = tbuf[k, pl.ds(j * TR, TR), :].astype(BF16)

    def row_copy(d, slot, src, dst, ss, rs):
        return pltpu.make_async_remote_copy(
            src_ref=src.at[d], dst_ref=dst.at[slot], send_sem=ss.at[d], recv_sem=rs.at[slot],
            device_id=(r, d), device_id_type=MESH,
        )

    def col_copy(d, slot, src, dst, ss, rs):
        return pltpu.make_async_remote_copy(
            src_ref=src.at[d], dst_ref=dst.at[slot], send_sem=ss.at[d], recv_sem=rs.at[slot],
            device_id=(d, c), device_id_type=MESH,
        )

    def send(copy, turn, me, count, *refs):
        def one(j, x):
            copy(turn(j), me, *refs).start()
            return x

        lax.fori_loop(1, count, one, 0)

    def receive(copy, turn, me, count, *refs):
        def one(j, x):
            copy(turn(j), turn(j), *refs).wait_recv()
            return x

        lax.fori_loop(1, count, one, 0)

    def finish(copy, turn, me, count, *refs):
        def one(j, x):
            copy(turn(j), me, *refs).wait_send()
            return x

        lax.fori_loop(1, count, one, 0)

    row_out = (row_copy, col, c, NC, sa, rl, rss, rrs)
    col_out = (col_copy, row, r, NR, sc, cl, css, crs)
    row_back = (row_copy, col, c, NC, rout, rres, rss2, rrs2)
    col_back = (col_copy, row, r, NR, cout, cres, css2, crs2)

    send(*row_out)
    send(*col_out)
    rl[c] = sa[c]
    cl[r] = sc[r]
    for load in loads[4:]:
        load.wait()

    pick_b = (iota((N, 44), 1) == iota((N, 44), 0) + RANK).astype(BF16)
    pick_c = (iota((44, T), 0) == (iota((44, T), 1) & 15) + RANK + N).astype(BF16)
    diagonal = (iota((T, T), 0) & 15) == (iota((T, T), 1) >> 4)

    def scan_line(ks):
        rates = []
        xb = linef[...].astype(BF16)
        for d, k in enumerate(ks):
            p = jnp.dot(xb, proj[k], preferred_element_type=F32)
            low = jnp.dot(p[:, :RANK], dtw[k], precision=lax.Precision.HIGHEST, preferred_element_type=F32)
            dt = softplus(low + dtb[k : k + 1, :])
            dts[d] = dt
            us[d] = dt * linef[...]
            pb = p.astype(BF16)
            bt = lax.dot_general(pick_b, pb, (((1,), (1,)), ((), ())), preferred_element_type=F32)
            for b in range(NB):
                bts[d, b] = bt[:, b * BL : (b + 1) * BL]
            ct = jnp.dot(pb, pick_c, preferred_element_type=F32)
            cms[d] = jnp.where(diagonal, ct, 0.0).astype(BF16)
            rates.append(jnp.exp(alog[k]) * (-LOG2E))

        def block(i, carry):
            h = list(carry)
            bs = (i, NB - 1 - i)
            base = [pl.multiple_of(b * BL, BL) for b in bs]
            maps = [bts[d, bs[d]] for d in (0, 1)]
            for step in range(BL):
                for d in (0, 1):
                    u = step if d == 0 else BL - 1 - step
                    dt = jnp.broadcast_to(dts[d, pl.ds(base[d] + u, 1), :], (8, E))
                    ux = jnp.broadcast_to(us[d, pl.ds(base[d] + u, 1), :], (8, E))
                    for half in (0, 1):
                        at = slice(half * 8, half * 8 + 8)
                        decay = jnp.exp2(dt * rates[d][at])
                        h[2 * d + half] = decay * h[2 * d + half] + ux * maps[d][at, u : u + 1]
                    both = jnp.concatenate([h[2 * d], h[2 * d + 1]], axis=0)
                    hst[d, u * N : (u + 1) * N, :] = both.astype(BF16)
            for d in (0, 1):
                ys[d, pl.ds(base[d], BL), :] = jnp.dot(
                    cms[d, pl.ds(base[d], BL), :], hst[d], preferred_element_type=F32
                )
            return tuple(h)

        zero = jnp.zeros((8, E), F32)
        lax.fori_loop(0, NB, block, (zero,) * 4)

    receive(*col_out)
    for j in range(NR):
        linef[pl.ds(j * TR, TR), :] = cl[j].astype(F32)
    scan_line((1, 3))
    for j in range(NR):
        at = pl.ds(j * TR, TR)
        cout[j] = (ys[0, at, :] + ys[1, at, :]).astype(BF16)
    send(*col_back)
    cres[r] = cout[r]

    receive(*row_out)
    for j in range(NC):
        linef[pl.ds(j * TC, TC), :] = rl[j].astype(F32)
    scan_line((0, 2))
    for j in range(NC):
        at = pl.ds(j * TC, TC)
        rout[j] = (ys[0, at, :] + ys[1, at, :]).astype(BF16)
    send(*row_back)
    rres[c] = rout[c]

    direct = skip[0:1, :] + skip[1:2, :] + skip[2:3, :] + skip[3:4, :]
    receive(*col_back)
    for j in range(TC):
        for k in range(3):
            tb2[k, pl.ds(j * TR, TR), :] = cres[j, :, pl.ds(k * 128, 128)].astype(F32)
    receive(*row_back)

    def total(q, x):
        at = pl.ds(pl.multiple_of(q * 8, 8), 8)
        parts = [tb2[k, pl.ds(q, 8, stride=TR), :] for k in range(3)]
        s = jnp.concatenate(parts, axis=1) + rres[q].astype(F32) + direct * sval[at, :]
        ys[0, at, :] = s
        return x

    lax.fori_loop(0, TR, total, 0, unroll=4)
    gated = (norm_rows(ys[0]) * gate[...]).astype(BF16)
    out_ref[...] = jnp.dot(gated, wout[...], preferred_element_type=F32).astype(BF16)

    for copy in halos:
        copy.wait_send()
    finish(*row_out)
    finish(*col_out)
    finish(*row_back)
    finish(*col_back)


def step(image, in_weight, conv_weight, conv_bias, proj_weight, dt_weight, dt_bias, a_log, skip_gain, out_weight):
    channels = image.shape[2]
    anywhere = pl.BlockSpec(memory_space=pl.ANY)
    vmem = pltpu.VMEM
    dma = pltpu.SemaphoreType.DMA
    bias = conv_bias.reshape(1, E)
    flat = image.reshape(T, channels)
    args = (image, flat, in_weight, conv_weight, bias, proj_weight, dt_weight, dt_bias, a_log, skip_gain, out_weight)
    result = pl.pallas_call(
        kernel,
        out_shape=jax.ShapeDtypeStruct((T, channels), BF16),
        in_specs=[anywhere] * len(args),
        out_specs=pl.BlockSpec(memory_space=pltpu.VMEM),
        scratch_shapes=[vmem(a.shape, a.dtype) for a in args[1:]]
        + [
            vmem((8, 8, channels), BF16),
            vmem((14, 8, channels), BF16),
            vmem((T + 16, E), F32),
            vmem((T + 16, E), F32),
            vmem((T + 16, E), F32),
            vmem((48, E), F32),
            vmem((48, E), F32),
            vmem((T, E), F32),
            vmem((3, T, 128), F32),
            vmem((T, E), F32),
            vmem((TR, TC, E), BF16),
            vmem((TC, TR, E), BF16),
            vmem((NC, TC, E), BF16),
            vmem((NR, TR, E), BF16),
            vmem((NC, TC, E), BF16),
            vmem((NR, TR, E), BF16),
            vmem((NC, TC, E), BF16),
            vmem((NR, TR, E), BF16),
            vmem((T, E), F32),
            vmem((2, T, E), F32),
            vmem((2, T, E), F32),
            vmem((2, NB, N, BL), F32),
            vmem((2, T, T), BF16),
            vmem((2, T, E), BF16),
            vmem((2, T, E), F32),
            vmem((3, T, 128), F32),
            vmem((2, T, 128), F32),
            dma((10,)), dma((8,)), dma((8,)),
            dma((NC,)), dma((NC,)), dma((NR,)), dma((NR,)),
            dma((NC,)), dma((NC,)), dma((NR,)), dma((NR,)),
        ],
        compiler_params=pltpu.CompilerParams(
            collective_id=0, has_side_effects=True, vmem_limit_bytes=48 * 1024 * 1024
        ),
    )(*args)
    return result.reshape(image.shape)


def solution(mesh):
    return jax.shard_map(
        step,
        mesh=mesh,
        in_specs=(P("rows", "cols", None), P(), P(), P(), P(), P(), P(), P(), P(), P()),
        out_specs=P("rows", "cols", None),
        check_vma=False,
    )
```

profile of v0, /device:TPU:1, one launch (start us, length us, event | category | flops | bytes accessed | tf_op | source)
XLA Modules:
  0.0 53.2 jit_solution(16351052953574758558)
XLA Ops:
  0.0 0.0 copy-start.6
  0.0 0.7 %reshape.10.cb_h = f32[1,384]{1,0:T(1,128)S(1)} reshape(f32[384]{0:T(512)} %param.13) | data formatting | bytes 3072 | tf_op jit(solution)/shard_map/reshape | solution.py:325
  0.7 0.9 %copy.12.dtw_h = f32[4,12,384]{2,1,0:T(8,128)S(1)} copy(f32[4,12,384]{2,0,1:T(4,128)} %param.15) | data formatting | bytes 147456 | tf_op args[5]
  1.6 0.0 copy-done.6
  1.6 0.0 copy-start.7
  1.6 0.0 copy-start.3
  1.7 0.0 copy-start.4
  1.7 0.0 copy-start.5
  1.7 0.1 copy.13.wout_h
  1.8 0.7 %copy-done.7 = bf16[4,384,44]{1,0,2:T(4,128)(2,1)S(1)} copy-done((bf16[4,384,44]{1,0,2:T(4,128)(2,1)S(1)}, bf16[4,384,44]{1,0,2:T(4,128)(2,1)}, u32[]{:S(2)}) %copy-start.7) | copy-done | bytes 135192
  2.5 0.0 copy-start
  2.5 0.0 copy-start.1
  2.5 0.0 copy-start.2
  2.5 0.3 copy.11.proj_h
  2.8 0.0 copy-done.3
  2.8 0.0 copy-done.4
  2.8 0.0 copy-done.5
  2.9 0.6 %copy-done = bf16[32,8,192]{2,1,0:T(8,128)(2,1)S(1)} copy-done((bf16[32,8,192]{2,1,0:T(8,128)(2,1)S(1)}, bf16[32,8,192]{2,1,0:T(8,128)(2,1)}, u32[]{:S(2)}) %copy-start) | copy-done | bytes 98328
  3.4 0.1 copy-done.1
  3.6 0.0 copy-done.2
  3.6 48.9 %shard_map.100 = bf16[256,192]{1,0:T(8,128)(2,1)S(1)} custom-call(bf16[32,8,192]{2,1,0:T(8,128)(2,1)S(1)} %copy-done, bf16[256,192]{1,0:T(8,128)(2,1)S(1)} %bitcast.2, bf16[192,768]{1,0:T(8,128)(2,1)S(1)} %copy-done.1, f32[3,3,384]{2,1,0:T(4,128)S(1)} %copy-done.3, f32[1,384]{1,0:T(1,128)S(1)} %reshape.10.cb_h, bf16[4,384,44]{2,1,0:T(8,128)(2,1)S(1)} %copy.11.proj_h, ...), custom_call_target="tpu_custom_call" | custom-call | tf_op jit(solution)/shard_map/pallas_call | solution.py:328
  52.5 0.7 %copy.15 = bf16[32,8,192]{2,1,0:T(8,128)(2,1)} copy(bf16[32,8,192]{2,1,0:T(8,128)(2,1)S(1)} %bitcast.3) | data formatting | bytes 196608
Async XLA Ops:
  0.0 1.6 %copy-start.6 = (bf16[384,192]{0,1:T(8,128)(2,1)S(1)}, bf16[384,192]{0,1:T(8,128)(2,1)}, u32[]{:S(2)}) copy-start(bf16[384,192]{0,1:T(8,128)(2,1)} %param.19) | copy-start | bytes 442372
  1.6 0.9 %copy-start.7 = (bf16[4,384,44]{1,0,2:T(4,128)(2,1)S(1)}, bf16[4,384,44]{1,0,2:T(4,128)(2,1)}, u32[]{:S(2)}) copy-start(bf16[4,384,44]{1,0,2:T(4,128)(2,1)} %param.14) | copy-start | bytes 405508
  1.6 1.2 %copy-start.3 = (f32[3,3,384]{2,1,0:T(4,128)S(1)}, f32[3,3,384]{2,1,0:T(4,128)}, u32[]{:S(2)}) copy-start(f32[3,3,384]{2,1,0:T(4,128)} %cw_h.1) | copy-start | bytes 41476
  1.7 1.2 %copy-start.4 = (f32[4,384]{1,0:T(4,128)S(1)}, f32[4,384]{1,0:T(4,128)}, u32[]{:S(2)}) copy-start(f32[4,384]{1,0:T(4,128)} %dtb_h.1) | copy-start | bytes 18436
  1.7 1.2 %copy-start.5 = (f32[4,384]{1,0:T(4,128)S(1)}, f32[4,384]{1,0:T(4,128)}, u32[]{:S(2)}) copy-start(f32[4,384]{1,0:T(4,128)} %skip_h.1) | copy-start | bytes 18436
  2.5 0.9 %copy-start = (bf16[32,8,192]{2,1,0:T(8,128)(2,1)S(1)}, bf16[32,8,192]{2,1,0:T(8,128)(2,1)}, u32[]{:S(2)}) copy-start(bf16[32,8,192]{2,1,0:T(8,128)(2,1)} %img3.1) | copy-start | bytes 294916
  2.5 1.0 %copy-start.1 = (bf16[192,768]{1,0:T(8,128)(2,1)S(1)}, bf16[192,768]{1,0:T(8,128)(2,1)}, u32[]{:S(2)}) copy-start(bf16[192,768]{1,0:T(8,128)(2,1)} %win_h.1) | copy-start | bytes 884740
  2.5 1.0 %copy-start.2 = (f32[4,16,384]{2,1,0:T(8,128)S(1)}, f32[4,16,384]{2,1,0:T(8,128)}, u32[]{:S(2)}) copy-start(f32[4,16,384]{2,1,0:T(8,128)} %alog_h.1) | copy-start | bytes 294916
where the time goes:
time: 53.3 us; the launch traced here: 53.2 us
  Pallas kernels  48.9 us (92%)
  local copies, waits for them, and re-layouts  4.16 us (8%)
    pallas_call x1, Pallas kernels, step(): pl.pallas_call(kernel, out_shape=jax.ShapeDtypeStruct((T, channels), BF16...  48.9 us
    unnamed x20, local copies, waits for them, and re-layouts  3.44 us

commit v1 on v0

--- a/solution.py
+++ b/solution.py
@@ -30,7 +30,8 @@
 
 
 def silu(v):
-    return v / (1.0 + jnp.exp(-v))
+    w = 0.5 * v
+    return w + w * jnp.tanh(w)
 
 
 def softplus(v):
@@ -47,7 +48,7 @@
     imgv, win, cw, cb, proj, dtw, dtb, alog, skip, wout,
     ecol, hal, xc, xl, xr, lh, rh, gate, tbuf, sval,
     sa, sc, rl, cl, rout, cout, rres, cres,
-    linef, dts, us, bts, cms, hst, ys, tb2, imgf,
+    linef, dts, us, rts, bts, cms, hst, ys, tb2, imgf, tot,
     wsem, hss, hrs, rss, rrs, css, crs, rss2, rrs2, css2, crs2,
 ):
     r = lax.axis_index("rows")
@@ -162,7 +163,7 @@
     loads[3].wait()
 
     def conv(q, x):
-        acc = jnp.broadcast_to(cb[...], (8, E))
+        acc = jnp.broadcast_to(cb[...].reshape(1, E), (8, E))
         for i in range(3):
             at = pl.ds(pl.multiple_of((q + i) * 8, 8), 8)
             for j, ref in enumerate((xl, xc, xr)):
@@ -175,7 +176,7 @@
             tbuf[k, pl.ds(q, 8, stride=TR), :] = sf[:, k * 128 : (k + 1) * 128]
         return x
 
-    lax.fori_loop(0, TR, conv, 0, unroll=2)
+    lax.fori_loop(0, TR, conv, 0, unroll=4)
     for j in range(TC):
         for k in range(3):
             sc[j, :, pl.ds(k * 128, 128)] = tbuf[k, pl.ds(j * TR, TR), :].astype(BF16)
@@ -230,25 +231,38 @@
     diagonal = (iota((T, T), 0) & 15) == (iota((T, T), 1) >> 4)
 
     def scan_line(ks):
-        rates = []
         xb = linef[...].astype(BF16)
         for d, k in enumerate(ks):
-            p = jnp.dot(xb, proj[k], preferred_element_type=F32)
-            low = jnp.dot(p[:, :RANK], dtw[k], precision=lax.Precision.HIGHEST, preferred_element_type=F32)
+            wk = proj[:, k, :].astype(BF16)
+            p = lax.dot_general(xb, wk, (((1,), (1,)), ((), ())), preferred_element_type=F32)
+            pb = p.astype(BF16)
+            rest = (p - pb.astype(F32)).astype(BF16)
+            w = dtw[:, k, :]
+            wb = w.astype(BF16)
+            wrest = (w - wb.astype(F32)).astype(BF16)
+            low = jnp.dot(pb[:, :RANK], wb, preferred_element_type=F32)
+            low = low + jnp.dot(rest[:, :RANK], wb, preferred_element_type=F32)
+            low = low + jnp.dot(pb[:, :RANK], wrest, preferred_element_type=F32)
             dt = softplus(low + dtb[k : k + 1, :])
             dts[d] = dt
             us[d] = dt * linef[...]
-            pb = p.astype(BF16)
             bt = lax.dot_general(pick_b, pb, (((1,), (1,)), ((), ())), preferred_element_type=F32)
             for b in range(NB):
                 bts[d, b] = bt[:, b * BL : (b + 1) * BL]
             ct = jnp.dot(pb, pick_c, preferred_element_type=F32)
             cms[d] = jnp.where(diagonal, ct, 0.0).astype(BF16)
-            rates.append(jnp.exp(alog[k]) * (-LOG2E))
-
-        def block(i, carry):
-            h = list(carry)
-            bs = (i, NB - 1 - i)
+            rts[d] = jnp.exp(alog[k]) * (-LOG2E)
+
+        def readout(slot, bs):
+            for d in (0, 1):
+                b = bs[d]
+                rows = pl.ds(pl.multiple_of(b * BL, BL), BL)
+                maps = cms[d, rows, :]
+                ys[d, pl.ds(pl.multiple_of((b + 1) * BL, BL), BL), :] = jnp.dot(
+                    maps, hst[d, slot], preferred_element_type=F32
+                )
+
+        def block(bs, slot, h):
             base = [pl.multiple_of(b * BL, BL) for b in bs]
             maps = [bts[d, bs[d]] for d in (0, 1)]
             for step in range(BL):
@@ -258,25 +272,34 @@
                     ux = jnp.broadcast_to(us[d, pl.ds(base[d] + u, 1), :], (8, E))
                     for half in (0, 1):
                         at = slice(half * 8, half * 8 + 8)
-                        decay = jnp.exp2(dt * rates[d][at])
+                        decay = jnp.exp2(dt * rts[d, at, :])
                         h[2 * d + half] = decay * h[2 * d + half] + ux * maps[d][at, u : u + 1]
                     both = jnp.concatenate([h[2 * d], h[2 * d + 1]], axis=0)
-                    hst[d, u * N : (u + 1) * N, :] = both.astype(BF16)
-            for d in (0, 1):
-                ys[d, pl.ds(base[d], BL), :] = jnp.dot(
-                    cms[d, pl.ds(base[d], BL), :], hst[d], preferred_element_type=F32
-                )
+                    hst[d, slot, u * N : (u + 1) * N, :] = both.astype(BF16)
+
+        def pair(i, carry):
+            h = list(carry)
+            b = 2 * i
+
+            @pl.when(i > 0)
+            def _():
+                readout(1, (b - 1, NB - b))
+
+            block((b, NB - 1 - b), 0, h)
+            readout(0, (b, NB - 1 - b))
+            block((b + 1, NB - 2 - b), 1, h)
             return tuple(h)
 
         zero = jnp.zeros((8, E), F32)
-        lax.fori_loop(0, NB, block, (zero,) * 4)
+        lax.fori_loop(0, NB // 2, pair, (zero,) * 4)
+        readout(1, (NB - 1, 0))
 
     receive(*col_out)
     for j in range(NR):
         linef[pl.ds(j * TR, TR), :] = cl[j].astype(F32)
     scan_line((1, 3))
     for j in range(NR):
-        at = pl.ds(j * TR, TR)
+        at = pl.ds(BL + j * TR, TR)
         cout[j] = (ys[0, at, :] + ys[1, at, :]).astype(BF16)
     send(*col_back)
     cres[r] = cout[r]
@@ -286,7 +309,7 @@
         linef[pl.ds(j * TC, TC), :] = rl[j].astype(F32)
     scan_line((0, 2))
     for j in range(NC):
-        at = pl.ds(j * TC, TC)
+        at = pl.ds(BL + j * TC, TC)
         rout[j] = (ys[0, at, :] + ys[1, at, :]).astype(BF16)
     send(*row_back)
     rres[c] = rout[c]
@@ -302,12 +325,13 @@
         at = pl.ds(pl.multiple_of(q * 8, 8), 8)
         parts = [tb2[k, pl.ds(q, 8, stride=TR), :] for k in range(3)]
         s = jnp.concatenate(parts, axis=1) + rres[q].astype(F32) + direct * sval[at, :]
-        ys[0, at, :] = s
+        tot[at, :] = s
         return x
 
     lax.fori_loop(0, TR, total, 0, unroll=4)
-    gated = (norm_rows(ys[0]) * gate[...]).astype(BF16)
-    out_ref[...] = jnp.dot(gated, wout[...], preferred_element_type=F32).astype(BF16)
+    gated = (norm_rows(tot[...]) * gate[...]).astype(BF16)
+    mixed = lax.dot_general(gated, wout[...], (((1,), (1,)), ((), ())), preferred_element_type=F32)
+    out_ref[...] = mixed.astype(BF16)
 
     for copy in halos:
         copy.wait_send()
@@ -322,9 +346,11 @@
     anywhere = pl.BlockSpec(memory_space=pl.ANY)
     vmem = pltpu.VMEM
     dma = pltpu.SemaphoreType.DMA
-    bias = conv_bias.reshape(1, E)
     flat = image.reshape(T, channels)
-    args = (image, flat, in_weight, conv_weight, bias, proj_weight, dt_weight, dt_bias, a_log, skip_gain, out_weight)
+    maps = jnp.transpose(proj_weight, (2, 0, 1))
+    low = jnp.transpose(dt_weight, (1, 0, 2))
+    back = jnp.transpose(out_weight, (1, 0))
+    args = (image, flat, in_weight, conv_weight, conv_bias, maps, low, dt_bias, a_log, skip_gain, back)
     result = pl.pallas_call(
         kernel,
         out_shape=jax.ShapeDtypeStruct((T, channels), BF16),
@@ -353,18 +379,20 @@
             vmem((T, E), F32),
             vmem((2, T, E), F32),
             vmem((2, T, E), F32),
+            vmem((2, N, E), F32),
             vmem((2, NB, N, BL), F32),
             vmem((2, T, T), BF16),
-            vmem((2, T, E), BF16),
-            vmem((2, T, E), F32),
+            vmem((2, 2, T, E), BF16),
+            vmem((2, T + 2 * BL, E), F32),
             vmem((3, T, 128), F32),
             vmem((2, T, 128), F32),
+            vmem((T, E), F32),
             dma((10,)), dma((8,)), dma((8,)),
             dma((NC,)), dma((NC,)), dma((NR,)), dma((NR,)),
             dma((NC,)), dma((NC,)), dma((NR,)), dma((NR,)),
         ],
         compiler_params=pltpu.CompilerParams(
-            collective_id=0, has_side_effects=True, vmem_limit_bytes=48 * 1024 * 1024
+            collective_id=0, has_side_effects=True, vmem_limit_bytes=62 * 1024 * 1024
         ),
     )(*args)
     return result.reshape(image.shape)

time: 53.3 us -> 47.8 us (0.90)
  Pallas kernels: 48.9 us -> 46.1 us
  local copies, waits for them, and re-layouts: 4.16 us -> 1.57 us
    pallas_call x1, Pallas kernels: 48.9 us -> 46.1 us  [step(): pl.pallas_call(kernel, out_shape=jax.ShapeDtypeStruct((T, channels), BF16...]
    unnamed x20 -> x1, local copies, waits for them, and re-layouts: 3.44 us -> 1.57 us
    reshape x1 -> x0, local copies, waits for them, and re-layouts: 0.72 us -> none  [step(): bias = conv_bias.reshape(1, E)]
where the time goes in v1:
time: 47.8 us; the launch traced here: 47.7 us
  Pallas kernels  46.1 us (96%)
  local copies, waits for them, and re-layouts  1.57 us (3%)
    pallas_call x1, Pallas kernels, step(): pl.pallas_call(kernel, out_shape=jax.ShapeDtypeStruct((T, channels), BF16...  46.1 us
    unnamed x1, local copies, waits for them, and re-layouts  1.57 us

profile of v1, /device:TPU:1, one launch (start us, length us, event | category | flops | bytes accessed | tf_op | source)
XLA Modules:
  0.0 47.7 jit_solution(13059236851372257665)
XLA Ops:
  0.0 46.1 %shard_map.100 = bf16[256,192]{1,0:T(8,128)(2,1)} custom-call(bf16[32,8,192]{2,1,0:T(8,128)(2,1)} %img3.1, bf16[256,192]{1,0:T(8,128)(2,1)} %bitcast.5, bf16[192,768]{1,0:T(8,128)(2,1)} %win_h.1, f32[3,3,384]{2,1,0:T(4,128)} %cw_h.1, f32[384]{0:T(512)} %cb_h.1, bf16[44,4,384]{2,1,0:T(4,128)(2,1)} %bitcast.8, f32[12,4,384]{2,1,0:T(4,128)} %bitcast.9, ...), custom_call_target="tpu_custom_call" | custom-call | tf_op jit(solution)/shard_map/pallas_call | solution.py:354
  46.1 1.6 %copy.12 = bf16[32,8,192]{2,1,0:T(8,128)(2,1)} copy(bf16[32,8,192]{2,1,0:T(8,128)(2,1)} %bitcast.6) | data formatting | bytes 196608

commit v2 on v1

--- a/solution.py
+++ b/solution.py
@@ -19,6 +19,7 @@
 E = 384
 N = 16
 RANK = 12
+KP = 3 * RANK + 2 * N
 BL = 16
 NB = T // BL
 
@@ -48,7 +49,7 @@
     imgv, win, cw, cb, proj, dtw, dtb, alog, skip, wout,
     ecol, hal, xc, xl, xr, lh, rh, gate, tbuf, sval,
     sa, sc, rl, cl, rout, cout, rres, cres,
-    linef, dts, us, rts, bts, cms, hst, ys, tb2, imgf, tot,
+    linef, dts, us, rts, wf, tf, wks, wds, bts, cms, hst, ys, tb2, imgf, tot,
     wsem, hss, hrs, rss, rrs, css, crs, rss2, rrs2, css2, crs2,
 ):
     r = lax.axis_index("rows")
@@ -95,12 +96,6 @@
         edge = jnp.concatenate([imgf[0, at, :], imgf[1, at, :]], axis=1)[:, : 128 + rest]
         for k in range(4):
             ecol[side * 4 + k] = edge[k * 8 : (k + 1) * 8].astype(BF16)
-
-    loads[1].wait()
-    normed = norm_rows(pixels).astype(BF16)
-    hidden = jnp.dot(normed, win[...], preferred_element_type=F32)
-    xc[pl.ds(8, T), :] = hidden[:, :E].astype(BF16).astype(F32)
-    gate[...] = silu(hidden[:, E:].astype(BF16).astype(F32))
 
     pl.semaphore_wait(barrier, (NC - 1) + (NR - 1) + 4)
 
@@ -123,6 +118,30 @@
     ]
     for copy in halos:
         copy.start()
+
+    loads[1].wait()
+    normed = norm_rows(pixels).astype(BF16)
+    hidden = jnp.dot(normed, win[...], preferred_element_type=F32)
+    xc[pl.ds(8, T), :] = hidden[:, :E].astype(BF16).astype(F32)
+    gate[...] = silu(hidden[:, E:].astype(BF16).astype(F32))
+
+
+    for load in (loads[4], loads[5], loads[7]):
+        load.wait()
+    for k in range(4):
+        wide = proj[:, k, :].astype(F32)
+        for copy in range(3):
+            wf[k, copy * RANK : (copy + 1) * RANK, :] = wide[:RANK]
+        wf[k, 3 * RANK : 3 * RANK + 2 * N, :] = wide[RANK:]
+        wks[k] = wf[k].astype(BF16)
+        w = dtw[:, k, :]
+        top = w.astype(BF16).astype(F32)
+        tf[k, 0:RANK, :] = top
+        tf[k, RANK : 2 * RANK, :] = top
+        tf[k, 2 * RANK : 3 * RANK, :] = w - top
+        wds[k] = tf[k].astype(BF16)
+        rts[k] = jnp.exp(alog[k]) * (-LOG2E)
+
     for copy in halos:
         copy.wait_recv()
 
@@ -219,30 +238,26 @@
     row_back = (row_copy, col, c, NC, rout, rres, rss2, rrs2)
     col_back = (col_copy, row, r, NR, cout, cres, css2, crs2)
 
+    send(*col_out)
     send(*row_out)
-    send(*col_out)
     rl[c] = sa[c]
     cl[r] = sc[r]
-    for load in loads[4:]:
+    for load in (loads[6], loads[8], loads[9]):
         load.wait()
 
-    pick_b = (iota((N, 44), 1) == iota((N, 44), 0) + RANK).astype(BF16)
-    pick_c = (iota((44, T), 0) == (iota((44, T), 1) & 15) + RANK + N).astype(BF16)
-    diagonal = (iota((T, T), 0) & 15) == (iota((T, T), 1) >> 4)
-
-    def scan_line(ks):
+    pick_b = (iota((N, KP), 1) == iota((N, KP), 0) + 3 * RANK).astype(BF16)
+    pick_c = (iota((KP, T), 0) == (iota((KP, T), 1) & 15) + 3 * RANK + N).astype(BF16)
+    diagonal = (iota((BL, T), 0) == (iota((BL, T), 1) >> 4)).astype(F32)
+    lane = iota((T, KP), 1)
+    middle = jnp.logical_and(lane >= RANK, lane < 2 * RANK)
+
+    def scan_line(ks, ready):
         xb = linef[...].astype(BF16)
         for d, k in enumerate(ks):
-            wk = proj[:, k, :].astype(BF16)
-            p = lax.dot_general(xb, wk, (((1,), (1,)), ((), ())), preferred_element_type=F32)
+            p = lax.dot_general(xb, wks[k], (((1,), (1,)), ((), ())), preferred_element_type=F32)
             pb = p.astype(BF16)
-            rest = (p - pb.astype(F32)).astype(BF16)
-            w = dtw[:, k, :]
-            wb = w.astype(BF16)
-            wrest = (w - wb.astype(F32)).astype(BF16)
-            low = jnp.dot(pb[:, :RANK], wb, preferred_element_type=F32)
-            low = low + jnp.dot(rest[:, :RANK], wb, preferred_element_type=F32)
-            low = low + jnp.dot(pb[:, :RANK], wrest, preferred_element_type=F32)
+            parts = jnp.where(middle, p - pb.astype(F32), p).astype(BF16)
+            low = jnp.dot(parts[:, : 3 * RANK], wds[k], preferred_element_type=F32)
             dt = softplus(low + dtb[k : k + 1, :])
             dts[d] = dt
             us[d] = dt * linef[...]
@@ -250,13 +265,12 @@
             for b in range(NB):
                 bts[d, b] = bt[:, b * BL : (b + 1) * BL]
             ct = jnp.dot(pb, pick_c, preferred_element_type=F32)
-            cms[d] = jnp.where(diagonal, ct, 0.0).astype(BF16)
-            rts[d] = jnp.exp(alog[k]) * (-LOG2E)
+            cms[d] = (ct.reshape(NB, BL, T) * diagonal[None]).reshape(T, T).astype(BF16)
 
         def readout(slot, bs):
             for d in (0, 1):
                 b = bs[d]
-                rows = pl.ds(pl.multiple_of(b * BL, BL), BL)
+                rows = pl.ds(pl.multiple_of(jnp.clip(b, 0, NB - 1) * BL, BL), BL)
                 maps = cms[d, rows, :]
                 ys[d, pl.ds(pl.multiple_of((b + 1) * BL, BL), BL), :] = jnp.dot(
                     maps, hst[d, slot], preferred_element_type=F32
@@ -272,7 +286,7 @@
                     ux = jnp.broadcast_to(us[d, pl.ds(base[d] + u, 1), :], (8, E))
                     for half in (0, 1):
                         at = slice(half * 8, half * 8 + 8)
-                        decay = jnp.exp2(dt * rts[d, at, :])
+                        decay = jnp.exp2(dt * rts[ks[d], at, :])
                         h[2 * d + half] = decay * h[2 * d + half] + ux * maps[d][at, u : u + 1]
                     both = jnp.concatenate([h[2 * d], h[2 * d + 1]], axis=0)
                     hst[d, slot, u * N : (u + 1) * N, :] = both.astype(BF16)
@@ -281,23 +295,23 @@
             h = list(carry)
             b = 2 * i
 
-            @pl.when(i > 0)
-            def _():
-                readout(1, (b - 1, NB - b))
-
+            ready(b)
+            readout(1, (b - 1, NB - b))
             block((b, NB - 1 - b), 0, h)
             readout(0, (b, NB - 1 - b))
             block((b + 1, NB - 2 - b), 1, h)
             return tuple(h)
 
         zero = jnp.zeros((8, E), F32)
+        for d in (0, 1):
+            hst[d, 1] = jnp.zeros((T, E), BF16)
         lax.fori_loop(0, NB // 2, pair, (zero,) * 4)
         readout(1, (NB - 1, 0))
 
     receive(*col_out)
     for j in range(NR):
         linef[pl.ds(j * TR, TR), :] = cl[j].astype(F32)
-    scan_line((1, 3))
+    scan_line((1, 3), lambda b: None)
     for j in range(NR):
         at = pl.ds(BL + j * TR, TR)
         cout[j] = (ys[0, at, :] + ys[1, at, :]).astype(BF16)
@@ -307,11 +321,31 @@
     receive(*row_out)
     for j in range(NC):
         linef[pl.ds(j * TC, TC), :] = rl[j].astype(F32)
-    scan_line((0, 2))
-    for j in range(NC):
-        at = pl.ds(BL + j * TC, TC)
-        rout[j] = (ys[0, at, :] + ys[1, at, :]).astype(BF16)
-    send(*row_back)
+
+    def emit(x):
+        for part in range(2):
+            j = 2 * x + part
+            at = pl.ds(pl.multiple_of(BL + j * TC, TC), TC)
+            rout[j] = (ys[0, at, :] + ys[1, at, :]).astype(BF16)
+
+            @pl.when(j != c)
+            def _():
+                row_copy(j, c, rout, rres, rss2, rrs2).start()
+
+    def ready(b):
+        @pl.when(b > NB // 2)
+        def _():
+            emit(b - 2)
+            emit(NB + 1 - b)
+
+        @pl.when(b > NB // 2 + 2)
+        def _():
+            emit(b - 3)
+            emit(NB + 2 - b)
+
+    scan_line((0, 2), ready)
+    for x in (0, 15, 1, 14, 2, 13):
+        emit(x)
     rres[c] = rout[c]
 
     direct = skip[0:1, :] + skip[1:2, :] + skip[2:3, :] + skip[3:4, :]
@@ -319,16 +353,18 @@
     for j in range(TC):
         for k in range(3):
             tb2[k, pl.ds(j * TR, TR), :] = cres[j, :, pl.ds(k * 128, 128)].astype(F32)
-    receive(*row_back)
-
-    def total(q, x):
+
+    def local(q, x):
         at = pl.ds(pl.multiple_of(q * 8, 8), 8)
         parts = [tb2[k, pl.ds(q, 8, stride=TR), :] for k in range(3)]
-        s = jnp.concatenate(parts, axis=1) + rres[q].astype(F32) + direct * sval[at, :]
-        tot[at, :] = s
+        tot[at, :] = jnp.concatenate(parts, axis=1) + direct * sval[at, :]
         return x
 
-    lax.fori_loop(0, TR, total, 0, unroll=4)
+    lax.fori_loop(0, TR, local, 0, unroll=4)
+    receive(*row_back)
+    for q in range(TR):
+        at = pl.ds(q * 8, 8)
+        tot[at, :] = tot[at, :] + rres[q].astype(F32)
     gated = (norm_rows(tot[...]) * gate[...]).astype(BF16)
     mixed = lax.dot_general(gated, wout[...], (((1,), (1,)), ((), ())), preferred_element_type=F32)
     out_ref[...] = mixed.astype(BF16)
@@ -379,7 +415,11 @@
             vmem((T, E), F32),
             vmem((2, T, E), F32),
             vmem((2, T, E), F32),
-            vmem((2, N, E), F32),
+            vmem((4, N, E), F32),
+            vmem((4, KP, E), F32),
+            vmem((4, 3 * RANK, E), F32),
+            vmem((4, KP, E), BF16),
+            vmem((4, 3 * RANK, E), BF16),
             vmem((2, NB, N, BL), F32),
             vmem((2, T, T), BF16),
             vmem((2, 2, T, E), BF16),

time: 47.8 us -> 43.2 us (0.904)
  Pallas kernels: 46.1 us -> 41.5 us
    pallas_call x1, Pallas kernels: 46.1 us -> 41.5 us  [step(): pl.pallas_call(kernel, out_shape=jax.ShapeDtypeStruct((T, channels), BF16...]
where the time goes in v2:
time: 43.2 us; the launch traced here: 43.1 us
  Pallas kernels  41.5 us (96%)
  local copies, waits for them, and re-layouts  1.57 us (4%)
    pallas_call x1, Pallas kernels, step(): pl.pallas_call(kernel, out_shape=jax.ShapeDtypeStruct((T, channels), BF16...  41.5 us
    unnamed x1, local copies, waits for them, and re-layouts  1.57 us

profile of v2, /device:TPU:1, one launch (start us, length us, event | category | flops | bytes accessed | tf_op | source)
XLA Modules:
  0.0 43.1 jit_solution(3146758759134431036)
XLA Ops:
  0.0 41.5 %shard_map.100 = bf16[256,192]{1,0:T(8,128)(2,1)} custom-call(bf16[32,8,192]{2,1,0:T(8,128)(2,1)} %img3.1, bf16[256,192]{1,0:T(8,128)(2,1)} %bitcast.5, bf16[192,768]{1,0:T(8,128)(2,1)} %win_h.1, f32[3,3,384]{2,1,0:T(4,128)} %cw_h.1, f32[384]{0:T(512)} %cb_h.1, bf16[44,4,384]{2,1,0:T(4,128)(2,1)} %bitcast.8, f32[12,4,384]{2,1,0:T(4,128)} %bitcast.9, ...), custom_call_target="tpu_custom_call" | custom-call | tf_op jit(solution)/shard_map/pallas_call | solution.py:390
  41.5 1.6 %copy.12 = bf16[32,8,192]{2,1,0:T(8,128)(2,1)} copy(bf16[32,8,192]{2,1,0:T(8,128)(2,1)} %bitcast.6) | data formatting | bytes 196608
